TPU v7x, 32 devices: a whole 2x2x4 slice. The times are simulated.
32 devices in a mesh: dp: 4 (over z), tensor: 4 (over y, x), section: 2 (over core).
Axes of the slice: x: 2, y: 2, z: 4, core: 2. Of those that a mesh axis runs over, the one named last changes fastest.
Arguments:
- grads: bfloat16 [4, 2, 768, 768], P('dp', 'section', 'tensor'), may hold values from -6 to 6
- errors: float32 [4, 2, 768, 768], P('dp', 'section', 'tensor'), may hold values from -3 to 3
- q_prev: float32 [2, 768, 32], P('section'), may hold values from -0.21875 to 0.21875
- p_root: float32 [2, 32, 32], P('section')
- q_root: float32 [2, 32, 32], P('section')
- momentum: float32 [2, 768, 768], P('section', 'tensor')
- weights: float32 [2, 768, 768], P('section', 'tensor'), may hold values from -0.21875 to 0.21875
- vec_grads: float32 [4, 2, 3, 768], P('dp', 'section', None, 'tensor'), may hold values from -6 to 6
- vec_momentum: float32 [2, 3, 768], P('section', None, 'tensor'), may hold values from -6 to 6
- vec_params: float32 [2, 3, 768], P('section', None, 'tensor'), may hold values from -3 to 3
Outputs:
- errors_out: float32 [4, 2, 768, 768], P('dp', 'section', 'tensor')
- p_factor: float32 [2, 768, 32], P('section', 'tensor')
- q_factor: float32 [2, 768, 32], P('section')
- momentum_out: float32 [2, 768, 768], P('section', 'tensor')
- weights_out: float32 [2, 768, 768], P('section', 'tensor')
- vec_momentum_out: float32 [2, 3, 768], P('section', None, 'tensor')
- vec_params_out: float32 [2, 3, 768], P('section', None, 'tensor')
All inputs are finite; a program needn't handle non-finite values.
Results may differ from a plain program's by a relative error of at most 0.0003.
Values sent between devices are 32-bit elements; how exact they have to be, the bound alone decides.
A program may use at most 64 MiB of HBM per device.

v0:
```python
import jax
import jax.numpy as jnp
from jax import lax
from jax.sharding import PartitionSpec as P

D = 768
HIGH = lax.Precision.HIGHEST


def shards(
    grads, errors, q_prev, p_root, q_root, momentum, weights, vec_grads, vec_momentum, vec_params
):
    replicas = lax.axis_size("dp")
    vec_local = vec_grads[0, 0]
    vec_sum = lax.psum(vec_local, "dp")
    merged = grads[0, 0].astype(jnp.float32) + errors[0, 0]
    p_local = jnp.dot(merged, q_prev[0], precision=HIGH, preferred_element_type=jnp.float32)
    p_sum = lax.psum(p_local, "dp")
    p_factor = jnp.dot(p_sum, p_root[0], precision=HIGH, preferred_element_type=jnp.float32)
    q_partial = lax.dot_general(
        merged,
        p_factor,
        (((0,), (0,)), ((), ())),
        precision=HIGH,
        preferred_element_type=jnp.float32,
    )
    q_whole = lax.psum(q_partial, ("dp", "tensor"))
    q_factor = jnp.dot(q_whole, q_root[0], precision=HIGH, preferred_element_type=jnp.float32)
    approx = (
        lax.dot_general(
            p_factor,
            q_factor,
            (((1,), (1,)), ((), ())),
            precision=HIGH,
            preferred_element_type=jnp.float32,
        )
        / replicas
    )
    errors_out = merged - approx
    vec_mean = vec_sum / replicas
    momentum_out = 0.9 * momentum[0] + approx
    vec_momentum_out = 0.9 * vec_momentum[0] + vec_mean
    local_total = jnp.sum(momentum_out * momentum_out) + jnp.sum(
        vec_momentum_out * vec_momentum_out
    )
    total = lax.psum(local_total, ("tensor", "section"))
    scale = 0.05 / jnp.sqrt(total / (2 * D * D + 6 * D) + 1e-06)
    weights_out = weights[0] - scale * momentum_out
    vec_params_out = vec_params[0] - scale * vec_momentum_out
    return (
        errors_out[None, None],
        p_factor[None],
        q_factor[None],
        momentum_out[None],
        weights_out[None],
        vec_momentum_out[None],
        vec_params_out[None],
    )


def solution(mesh):
    in_specs = (
        P("dp", "section", "tensor", None),
        P("dp", "section", "tensor", None),
        P("section", None, None),
        P("section", None, None),
        P("section", None, None),
        P("section", "tensor", None),
        P("section", "tensor", None),
        P("dp", "section", None, "tensor"),
        P("section", None, "tensor"),
        P("section", None, "tensor"),
    )
    out_specs = (
        P("dp", "section", "tensor", None),
        P("section", "tensor", None),
        P("section", None, None),
        P("section", "tensor", None),
        P("section", "tensor", None),
        P("section", None, "tensor"),
        P("section", None, "tensor"),
    )
    return jax.shard_map(shards, mesh=mesh, in_specs=in_specs, out_specs=out_specs, check_vma=False)
```

profile of v0, /device:TPU:0, one launch (start us, length us, event | category | flops | bytes accessed | tf_op | source)
XLA Modules:
  0.0 168.7 jit_solution(3444834635649647149)
XLA Ops:
  7.2 0.0 copy-start
  7.2 0.0 all-reduce.3.cloned.1.call-start
  7.2 0.7 copy.26
  7.9 0.2 copy-done
  8.1 0.0 copy-start.1
  8.1 0.0 copy-start.2
  8.1 1.8 %fusion.3 = f32[192,32]{1,0:T(8,128)S(1)} fusion(f32[1,1,192,768]{3,2,1,0:T(8,128)} %param.11, bf16[1,1,192,768]{3,2,1,0:T(8,128)(2,1)} %param.10, f32[1,768,32]{1,2,0:T(8,128)S(1)} %copy-done), kind=kOutput, calls=%fused_computation.7 | convolution fusion | flops 56918016 | bytes 1007616 | tf_op jit(solution)/shard_map/dot_general | solution.py:17
  9.9 0.0 copy-start.7
  9.9 22.7 %all-reduce = (f32[192,32]{1,0:T(8,128)S(1)}, f32[3,192]{1,0:T(4,128)S(1)}) all-reduce(f32[192,32]{1,0:T(8,128)S(1)} %fusion.3, f32[3,192]{1,0:T(4,128)S(1)} %bitcast.52), channel_id=1, replica_groups=mesh['dp'=4,'tensor'=4,'section'=2] {'dp'}, use_global_device_ids=true, to_apply=%region_0.0 | all-reduce | flops 6720 | bytes 53760 | tf_op jit(solution)/shard_map/psum | solution.py:18
  32.6 0.0 copy-done.7
  32.6 0.3 fusion.9
  32.9 0.0 copy-done.1
  32.9 0.0 copy-done.2
  32.9 0.0 copy-start.6
  32.9 0.0 copy-start.9
  33.0 0.0 copy-start.8
  33.0 2.2 %fusion.1 = f32[768,32]{1,0:T(8,128)} fusion(f32[192,32]{0,1:T(8,128)S(1)} %fusion.9, f32[1,1,192,768]{3,2,1,0:T(8,128)S(1)} %copy-done.1, bf16[1,1,192,768]{3,2,1,0:T(8,128)(2,1)S(1)} %copy-done.2), kind=kOutput, calls=%fused_computation.5 | convolution fusion | flops 56918016 | bytes 1007616 | tf_op jit(solution)/shard_map/dot_general | solution.py:20
  35.2 0.0 copy-start.3
  35.2 0.0 all-reduce.3.cloned.1.call-update
  35.2 0.0 copy-done.9
  35.2 0.6 multiply_reduce_fusion.1
  35.8 105.7 %all-reduce.3.cloned.1.call-done = f32[768,32]{1,0:T(8,128)} async-done(((f32[768,32]{1,0:T(8,128)}), f32[768,32]{1,0:T(8,128)}) %all-reduce.3.cloned.1.call-update) | async-done | bytes 98320 | tf_op jit(solution)/shard_map/psum | solution.py:27
  141.5 0.0 copy-done.8
  141.5 1.5 fusion.7
  143.1 0.0 copy-done.6
  143.1 0.0 copy-done.3
  143.1 0.0 copy-start.5
  143.1 0.0 copy-start.4
  143.1 1.4 multiply_reduce_fusion
  144.5 0.0 copy-done.5
  145.8 0.6 broadcast_in_dim.26
  146.4 12.3 %psum.31 = f32[]{:T(128)} all-reduce(f32[]{:T(128)S(6)} %add.31), channel_id=1, replica_groups=mesh['dp'=4,'tensor'=4,'section'=2] {'tensor','section'}, use_global_device_ids=true, to_apply=%region_5.0 | all-reduce | flops 1 | bytes 8 | tf_op jit(solution)/shard_map/psum | solution.py:46
  159.3 0.0 copy-start.10
  159.3 0.6 copy-done.10
  160.0 0.6 broadcast_in_dim.27
  160.6 0.0 copy-done.4
  160.6 1.3 fusion
  (1 shorter events, 0.0 us)
Async XLA Ops:
  7.2 0.9 copy-start
  7.2 134.4 %all-reduce.3.cloned.1.call-start = ((), (), s32[]{:S(2)}) async-start(), calls=%async_computation | async-start | bytes 786432 | tf_op jit(solution)/shard_map/psum | solution.py:27
  8.1 24.8 %copy-start.1 = (f32[1,1,192,768]{3,2,1,0:T(8,128)S(1)}, f32[1,1,192,768]{3,2,1,0:T(8,128)}, u32[]{:S(2)}) copy-start(f32[1,1,192,768]{3,2,1,0:T(8,128)} %param.11) | copy-start | bytes 1769476
  8.1 24.9 %copy-start.2 = (bf16[1,1,192,768]{3,2,1,0:T(8,128)(2,1)S(1)}, bf16[1,1,192,768]{3,2,1,0:T(8,128)(2,1)}, u32[]{:S(2)}) copy-start(bf16[1,1,192,768]{3,2,1,0:T(8,128)(2,1)} %param.10) | copy-start | bytes 884740
  9.9 22.7 %copy-start.7 = (f32[1,32,32]{2,1,0:T(8,128)S(1)}, f32[1,32,32]{2,1,0:T(8,128)}, u32[]{:S(2)}) copy-start(f32[1,32,32]{2,1,0:T(8,128)} %param.13) | copy-start | bytes 12292
  32.9 110.1 %copy-start.6 = (f32[192,32]{0,1:T(8,128)}, f32[192,32]{0,1:T(8,128)S(1)}, u32[]{:S(2)}) copy-start(f32[192,32]{0,1:T(8,128)S(1)} %fusion.9) | copy-start | bytes 73732
  32.9 2.3 %copy-start.9 = (f32[1,3,192]{2,0,1:T(1,128)S(1)}, f32[1,3,192]{2,0,1:T(1,128)}, u32[]{:S(2)}) copy-start(f32[1,3,192]{2,0,1:T(1,128)} %param.18) | copy-start | bytes 6916
  33.0 108.6 %copy-start.8 = (f32[1,32,32]{2,1,0:T(8,128)S(1)}, f32[1,32,32]{2,1,0:T(8,128)}, u32[]{:S(2)}) copy-start(f32[1,32,32]{2,1,0:T(8,128)} %param.14) | copy-start | bytes 12292
  35.2 107.9 %copy-start.3 = (f32[1,192,768]{2,1,0:T(8,128)S(1)}, f32[1,192,768]{2,1,0:T(8,128)}, u32[]{:S(2)}) copy-start(f32[1,192,768]{2,1,0:T(8,128)} %param.15) | copy-start | bytes 1769476
  143.1 1.4 copy-start.5
  143.1 17.5 %copy-start.4 = (f32[1,192,768]{2,1,0:T(8,128)S(1)}, f32[1,192,768]{2,1,0:T(8,128)}, u32[]{:S(2)}) copy-start(f32[1,192,768]{2,1,0:T(8,128)} %param.16) | copy-start | bytes 1769476
  159.3 0.7 copy-start.10
Sparse Core Ops, SparseCore 0:
  35.3 106.1 all-reduce.2
where the time goes:
time: 169 us
  waiting for transfers between devices  106 us (63%)
  blocking collectives  35 us (21%)
  between operations  16.2 us (10%)
  matrix products  7.21 us (4%)
  local copies, waits for them, and re-layouts  2.7 us (2%)
  other arithmetic  1.89 us (1%)
    psum x1, waiting for transfers between devices, shards(): q_whole = lax.psum(q_partial, ('dp', 'tensor'))  106 us
    psum x1, blocking collectives, shards(): p_sum = lax.psum(p_local, 'dp')  22.7 us
    psum x1, blocking collectives, shards(): total = lax.psum(local_total, ('tensor', 'section'))  12.3 us
  transfers between devices with their start and end apart: 1, of which 1 were waited for; matrix products, arithmetic and copies ran while one was open for 0% of the time, Pallas kernels for 0%

commit v1 on v0

--- a/solution.py
+++ b/solution.py
@@ -24,7 +24,7 @@
         precision=HIGH,
         preferred_element_type=jnp.float32,
     )
-    q_whole = lax.psum(q_partial, ("dp", "tensor"))
+    q_whole = jnp.sum(lax.all_gather(q_partial, ("dp", "tensor")), axis=0)
     q_factor = jnp.dot(q_whole, q_root[0], precision=HIGH, preferred_element_type=jnp.float32)
     approx = (
         lax.dot_general(

time: 169 us -> 120 us (0.71)
  waiting for transfers between devices: 106 us -> 55.8 us
  local copies, waits for them, and re-layouts: 2.7 us -> 4.4 us
    psum x1 -> x0, waiting for transfers between devices: 106 us -> none  [shards(): q_whole = lax.psum(q_partial, ('dp', 'tensor'))]
    all_gather x0 -> x1, waiting for transfers between devices: none -> 55.8 us  [shards(): q_whole = jnp.sum(lax.all_gather(q_partial, ('dp', 'tensor')), axis=0)]
    unnamed x23 -> x22, local copies, waits for them, and re-layouts: 1.53 us -> 3.24 us
  transfers between devices with their start and end apart: 1 -> 1, of which waited for: 1 -> 1; matrix products, arithmetic and copies ran while one was open for 0% -> 1% of each run, Pallas kernels for 0% -> 0%
where the time goes in v1:
time: 120 us
  waiting for transfers between devices  55.8 us (46%)
  blocking collectives  35 us (29%)
  between operations  16.2 us (14%)
  matrix products  6.47 us (5%)
  local copies, waits for them, and re-layouts  4.4 us (4%)
  other arithmetic  2.13 us (2%)
    all_gather x1, waiting for transfers between devices, shards(): q_whole = jnp.sum(lax.all_gather(q_partial, ('dp', 'tensor')), axis=0)  55.8 us
    psum x1, blocking collectives, shards(): p_sum = lax.psum(p_local, 'dp')  22.7 us
    psum x1, blocking collectives, shards(): total = lax.psum(local_total, ('tensor', 'section'))  12.3 us
    unnamed x22, local copies, waits for them, and re-layouts  3.24 us
  transfers between devices with their start and end apart: 1, of which 1 were waited for; matrix products, arithmetic and copies ran while one was open for 1% of the time, Pallas kernels for 0%

profile of v1, /device:TPU:0, one launch (start us, length us, event | category | flops | bytes accessed | tf_op | source)
XLA Modules:
  0.0 119.9 jit_solution(13537530717081118306)
XLA Ops:
  7.2 0.0 copy-start
  7.2 0.0 copy-start.1
  7.2 0.0 copy-start.8
  7.2 0.0 all-gather.3.cloned.1.call-start
  7.2 0.7 copy.28
  8.0 0.1 copy-done
  8.1 1.7 %fusion.3 = f32[192,32]{1,0:T(8,128)S(1)} fusion(f32[1,1,192,768]{3,2,1,0:T(8,128)} %param.11, bf16[1,1,192,768]{3,2,1,0:T(8,128)(2,1)} %param.10, f32[1,768,32]{1,2,0:T(8,128)S(1)} %copy-done), kind=kOutput, calls=%fused_computation.8 | convolution fusion | flops 56918016 | bytes 1007616 | tf_op jit(solution)/shard_map/dot_general | solution.py:17
  9.8 22.7 %all-reduce = (f32[192,32]{1,0:T(8,128)S(1)}, f32[3,192]{1,0:T(4,128)S(1)}) all-reduce(f32[192,32]{1,0:T(8,128)S(1)} %fusion.3, f32[3,192]{1,0:T(4,128)S(1)} %bitcast.58), channel_id=1, replica_groups=mesh['dp'=4,'tensor'=4,'section'=2] {'dp'}, use_global_device_ids=true, to_apply=%region_0.0 | all-reduce | flops 6720 | bytes 53760 | tf_op jit(solution)/shard_map/psum | solution.py:18
  32.5 1.0 fusion.9
  33.5 0.0 copy-done.1
  33.5 0.0 copy-start.6
  33.5 2.1 %fusion.1 = f32[768,32]{0,1:T(8,128)} fusion(f32[192,32]{0,1:T(8,128)S(1)} %fusion.9, f32[1,1,192,768]{3,2,1,0:T(8,128)S(1)} %copy-done.1, bf16[1,1,192,768]{3,2,1,0:T(8,128)(2,1)} %param.10), kind=kOutput, calls=%fused_computation.6 | convolution fusion | flops 56918016 | bytes 1007616 | tf_op jit(solution)/shard_map/dot_general | solution.py:20
  35.6 0.0 all-gather.3.cloned.1.call-update
  35.6 0.0 copy-done.8
  35.7 0.6 multiply_reduce_fusion.1
  36.3 55.8 %all-gather.3.cloned.1.call-done = f32[12288,32]{0,1:T(8,128)} async-done(((f32[768,32]{0,1:T(8,128)}), f32[12288,32]{0,1:T(8,128)}) %all-gather.3.cloned.1.call-update) | async-done | bytes 1572880 | tf_op jit(solution)/shard_map/all_gather | solution.py:27
  92.0 1.9 %copy.21 = f32[4,8,16,768]{3,2,1,0:T(8,128)S(1)} copy(f32[4,8,16,768]{3,1,2,0:T(8,128)} %bitcast.55) | data formatting | bytes 3145728
  93.9 0.0 copy-start.7
  93.9 0.0 copy-start.3
  93.9 0.0 copy-start.9
  93.9 0.0 copy-start.2
  94.0 0.0 copy-start.4
  94.0 0.2 bitcast_reduce_fusion
  94.2 0.4 copy-done.7
  94.6 0.3 fusion.7
  94.9 0.0 copy-done.6
  94.9 0.1 copy-done.3
  95.0 0.0 copy-start.5
  95.0 1.4 %multiply_reduce_fusion = (f32[]{:T(128)}, f32[192,768]{1,0:T(8,128)S(1)}) fusion(f32[1,192,768]{2,1,0:T(8,128)S(1)} %copy-done.3, f32[192,32]{0,1:T(8,128)S(1)} %fusion.9, f32[768,32]{0,1:T(8,128)S(1)} %fusion.7), kind=kOutput, calls=%fused_computation.11 | convolution fusion | flops 57360384 | bytes 1302532 | tf_op jit(solution)/shard_map/dot_general | solution.py:30
  97.6 0.6 broadcast_in_dim.26
  98.2 12.3 %psum.23 = f32[]{:T(128)} all-reduce(f32[]{:T(128)S(6)} %add.29), channel_id=1, replica_groups=mesh['dp'=4,'tensor'=4,'section'=2] {'tensor','section'}, use_global_device_ids=true, to_apply=%region_5.0 | all-reduce | flops 1 | bytes 8 | tf_op jit(solution)/shard_map/psum | solution.py:46
  111.2 0.0 copy-done.9
  111.2 0.6 broadcast_in_dim.27
  111.8 0.0 copy-done.2
  111.8 0.0 copy-done.4
  111.8 1.3 %fusion = (f32[1,192,768]{2,1,0:T(8,128)}, f32[1,192,768]{2,1,0:T(8,128)}, f32[1,1,192,768]{3,2,1,0:T(8,128)}) fusion(f32[1,192,768]{2,1,0:T(8,128)S(1)} %copy-done.4, f32[]{:T(128)S(6)} %div.23, f32[192,768]{1,0:T(8,128)S(1)} %get-tuple-element.15, f32[1,192,768]{2,1,0:T(8,128)S(1)} %copy-done.3, f32[1,1,192,768]{3,2,1,0:T(8,128)S(1)} %copy-done.1, ...), kind=kLoop, calls=%fused_computation.3 | loop fusion | flops 1032192 | bytes 4423684 | tf_op jit(solution)/shard_map/broadcast_in_dim | solution.py:55
  113.1 0.0 copy-done.5
  (1 shorter events, 0.0 us)
Async XLA Ops:
  7.2 0.9 copy-start
  7.2 26.3 %copy-start.1 = (f32[1,1,192,768]{3,2,1,0:T(8,128)S(1)}, f32[1,1,192,768]{3,2,1,0:T(8,128)}, u32[]{:S(2)}) copy-start(f32[1,1,192,768]{3,2,1,0:T(8,128)} %param.11) | copy-start | bytes 1769476
  7.2 28.5 %copy-start.8 = (f32[1,3,192]{2,0,1:T(1,128)S(1)}, f32[1,3,192]{2,0,1:T(1,128)}, u32[]{:S(2)}) copy-start(f32[1,3,192]{2,0,1:T(1,128)} %param.18) | copy-start | bytes 6916
  7.2 84.8 %all-gather.3.cloned.1.call-start = ((), (), s32[]{:S(2)}) async-start(), calls=%async_computation | async-start | bytes 1671168 | tf_op jit(solution)/shard_map/all_gather | solution.py:27
  33.5 61.4 %copy-start.6 = (f32[192,32]{0,1:T(8,128)}, f32[192,32]{0,1:T(8,128)S(1)}, u32[]{:S(2)}) copy-start(f32[192,32]{0,1:T(8,128)S(1)} %fusion.9) | copy-start | bytes 73732
  93.9 0.7 copy-start.7
  93.9 1.1 copy-start.3
  93.9 17.3 %copy-start.9 = (f32[1,3,192]{2,0,1:T(1,128)S(1)}, f32[1,3,192]{2,0,1:T(1,128)}, u32[]{:S(2)}) copy-start(f32[1,3,192]{2,0,1:T(1,128)} %param.19) | copy-start | bytes 6916
  93.9 17.9 %copy-start.2 = (bf16[1,1,192,768]{3,2,1,0:T(8,128)(2,1)S(1)}, bf16[1,1,192,768]{3,2,1,0:T(8,128)(2,1)}, u32[]{:S(2)}) copy-start(bf16[1,1,192,768]{3,2,1,0:T(8,128)(2,1)} %param.10) | copy-start | bytes 884740
  94.0 17.9 %copy-start.4 = (f32[1,192,768]{2,1,0:T(8,128)S(1)}, f32[1,192,768]{2,1,0:T(8,128)}, u32[]{:S(2)}) copy-start(f32[1,192,768]{2,1,0:T(8,128)} %param.16) | copy-start | bytes 1769476
  95.0 18.1 %copy-start.5 = (f32[768,32]{0,1:T(8,128)}, f32[768,32]{0,1:T(8,128)S(1)}, u32[]{:S(2)}) copy-start(f32[768,32]{0,1:T(8,128)S(1)} %fusion.7) | copy-start | bytes 294916
Sparse Core Ops, SparseCore 0:
  35.8 56.2 all-gather.2

commit v2 on v0

--- a/solution.py
+++ b/solution.py
@@ -24,7 +24,7 @@
         precision=HIGH,
         preferred_element_type=jnp.float32,
     )
-    q_whole = lax.psum(q_partial, ("dp", "tensor"))
+    q_whole = lax.psum(lax.psum(q_partial, "tensor"), "dp")
     q_factor = jnp.dot(q_whole, q_root[0], precision=HIGH, preferred_element_type=jnp.float32)
     approx = (
         lax.dot_general(

time: 169 us -> 145 us (0.86)
  waiting for transfers between devices: 106 us -> 80.8 us
    psum x1 -> x2, waiting for transfers between devices: 106 us -> 80.8 us  [shards(): q_whole = lax.psum(lax.psum(q_partial, 'tensor'), 'dp')]
  transfers between devices with their start and end apart: 1 -> 2, of which waited for: 1 -> 2; matrix products, arithmetic and copies ran while one was open for 0% -> 0% of each run, Pallas kernels for 0% -> 0%
where the time goes in v2:
time: 145 us
  waiting for transfers between devices  80.8 us (56%)
  blocking collectives  35.1 us (24%)
  between operations  16.2 us (11%)
  matrix products  7.21 us (5%)
  local copies, waits for them, and re-layouts  3.35 us (2%)
  other arithmetic  1.89 us (1%)
    psum x2, waiting for transfers between devices, shards(): q_whole = lax.psum(lax.psum(q_partial, 'tensor'), 'dp')  80.8 us
    psum x1, blocking collectives, shards(): p_sum = lax.psum(p_local, 'dp')  22.7 us
    psum x1, blocking collectives, shards(): total = lax.psum(local_total, ('tensor', 'section'))  12.4 us
  transfers between devices with their start and end apart: 2, of which 2 were waited for; matrix products, arithmetic and copies ran while one was open for 0% of the time, Pallas kernels for 0%

profile of v2, /device:TPU:0, one launch (start us, length us, event | category | flops | bytes accessed | tf_op | source)
XLA Modules:
  0.0 144.6 jit_solution(6738236280038735940)
XLA Ops:
  7.2 0.0 copy-start
  7.2 0.0 all-reduce.4.cloned.1.call-start
  7.2 0.7 copy.26
  7.9 0.2 copy-done
  8.1 0.0 copy-start.1
  8.1 0.0 copy-start.2
  8.1 1.8 %fusion.3 = f32[192,32]{1,0:T(8,128)S(1)} fusion(f32[1,1,192,768]{3,2,1,0:T(8,128)} %param.11, bf16[1,1,192,768]{3,2,1,0:T(8,128)(2,1)} %param.10, f32[1,768,32]{1,2,0:T(8,128)S(1)} %copy-done), kind=kOutput, calls=%fused_computation.7 | convolution fusion | flops 56918016 | bytes 1007616 | tf_op jit(solution)/shard_map/dot_general | solution.py:17
  9.9 0.0 copy-start.7
  9.9 22.7 %all-reduce = (f32[192,32]{1,0:T(8,128)S(1)}, f32[3,192]{1,0:T(4,128)S(1)}) all-reduce(f32[192,32]{1,0:T(8,128)S(1)} %fusion.3, f32[3,192]{1,0:T(4,128)S(1)} %bitcast.52), channel_id=1, replica_groups=mesh['dp'=4,'tensor'=4,'section'=2] {'dp'}, use_global_device_ids=true, to_apply=%region_0.0 | all-reduce | flops 6720 | bytes 53760 | tf_op jit(solution)/shard_map/psum | solution.py:18
  32.6 0.0 copy-done.7
  32.6 0.3 fusion.9
  32.9 0.0 copy-done.1
  32.9 0.0 copy-done.2
  32.9 0.0 copy-start.6
  32.9 2.2 %fusion.1 = f32[768,32]{1,0:T(8,128)} fusion(f32[192,32]{0,1:T(8,128)S(1)} %fusion.9, f32[1,1,192,768]{3,2,1,0:T(8,128)S(1)} %copy-done.1, bf16[1,1,192,768]{3,2,1,0:T(8,128)(2,1)S(1)} %copy-done.2), kind=kOutput, calls=%fused_computation.5 | convolution fusion | flops 56918016 | bytes 1007616 | tf_op jit(solution)/shard_map/dot_general | solution.py:20
  35.1 0.0 copy-start.3
  35.1 0.0 all-reduce.4.cloned.1.call-update
  35.2 0.0 all-reduce.6.cloned.1.call-start
  35.2 42.5 %all-reduce.4.cloned.1.call-done = f32[768,32]{1,0:T(8,128)} async-done(((f32[768,32]{1,0:T(8,128)}), f32[768,32]{1,0:T(8,128)}) %all-reduce.4.cloned.1.call-update) | async-done | bytes 98320 | tf_op jit(solution)/shard_map/psum | solution.py:27
  77.7 0.0 copy-start.9
  77.7 0.0 copy-start.8
  77.7 0.0 all-reduce.6.cloned.1.call-update
  77.8 0.7 copy-done.9
  78.4 0.6 multiply_reduce_fusion.1
  79.0 38.3 %all-reduce.6.cloned.1.call-done = f32[768,32]{1,0:T(8,128)} async-done(((f32[768,32]{1,0:T(8,128)}), f32[768,32]{1,0:T(8,128)}) %all-reduce.6.cloned.1.call-update) | async-done | bytes 98320 | tf_op jit(solution)/shard_map/psum | solution.py:27
  117.3 0.0 copy-done.8
  117.3 1.5 %fusion.7 = f32[768,32]{0,1:T(8,128)S(1)} fusion(f32[768,32]{1,0:T(8,128)} %all-reduce.6.cloned.1.call-done, f32[1,32,32]{2,1,0:T(8,128)S(1)} %copy-done.8), kind=kOutput, calls=%fused_computation.13 | convolution fusion | flops 9437184 | bytes 200704 | tf_op jit(solution)/shard_map/dot_general | solution.py:28
  118.8 0.0 copy-done.6
  118.8 0.0 copy-done.3
  118.9 0.0 copy-start.5
  118.9 0.0 copy-start.4
  118.9 1.4 multiply_reduce_fusion
  120.2 0.0 copy-done.5
  121.5 0.6 broadcast_in_dim.26
  122.1 12.4 %psum.39 = f32[]{:T(128)} all-reduce(f32[]{:T(128)S(6)} %add.33), channel_id=1, replica_groups=mesh['dp'=4,'tensor'=4,'section'=2] {'tensor','section'}, use_global_device_ids=true, to_apply=%region_6.0 | all-reduce | flops 1 | bytes 8 | tf_op jit(solution)/shard_map/psum | solution.py:46
  135.2 0.0 copy-start.10
  135.2 0.6 copy-done.10
  135.9 0.6 broadcast_in_dim.27
  136.4 0.0 copy-done.4
  136.4 1.3 fusion
  (1 shorter events, 0.0 us)
Async XLA Ops:
  7.2 0.9 copy-start
  7.2 70.6 %all-reduce.4.cloned.1.call-start = ((), (), s32[]{:S(2)}) async-start(), calls=%async_computation | async-start | bytes 786432 | tf_op jit(solution)/shard_map/psum | solution.py:27
  8.1 24.8 %copy-start.1 = (f32[1,1,192,768]{3,2,1,0:T(8,128)S(1)}, f32[1,1,192,768]{3,2,1,0:T(8,128)}, u32[]{:S(2)}) copy-start(f32[1,1,192,768]{3,2,1,0:T(8,128)} %param.11) | copy-start | bytes 1769476
  8.1 24.9 %copy-start.2 = (bf16[1,1,192,768]{3,2,1,0:T(8,128)(2,1)S(1)}, bf16[1,1,192,768]{3,2,1,0:T(8,128)(2,1)}, u32[]{:S(2)}) copy-start(bf16[1,1,192,768]{3,2,1,0:T(8,128)(2,1)} %param.10) | copy-start | bytes 884740
  9.9 22.7 %copy-start.7 = (f32[1,32,32]{2,1,0:T(8,128)S(1)}, f32[1,32,32]{2,1,0:T(8,128)}, u32[]{:S(2)}) copy-start(f32[1,32,32]{2,1,0:T(8,128)} %param.13) | copy-start | bytes 12292
  32.9 85.9 %copy-start.6 = (f32[192,32]{0,1:T(8,128)}, f32[192,32]{0,1:T(8,128)S(1)}, u32[]{:S(2)}) copy-start(f32[192,32]{0,1:T(8,128)S(1)} %fusion.9) | copy-start | bytes 73732
  35.1 83.7 %copy-start.3 = (f32[1,192,768]{2,1,0:T(8,128)S(1)}, f32[1,192,768]{2,1,0:T(8,128)}, u32[]{:S(2)}) copy-start(f32[1,192,768]{2,1,0:T(8,128)} %param.15) | copy-start | bytes 1769476
  35.2 82.1 %all-reduce.6.cloned.1.call-start = ((), (), s32[]{:S(2)}) async-start(), calls=%async_computation.1 | async-start | bytes 786432 | tf_op jit(solution)/shard_map/psum | solution.py:27
  77.7 0.7 copy-start.9
  77.7 39.6 %copy-start.8 = (f32[1,32,32]{2,1,0:T(8,128)S(1)}, f32[1,32,32]{2,1,0:T(8,128)}, u32[]{:S(2)}) copy-start(f32[1,32,32]{2,1,0:T(8,128)} %param.14) | copy-start | bytes 12292
  118.9 1.4 copy-start.5
  118.9 17.6 %copy-start.4 = (f32[1,192,768]{2,1,0:T(8,128)S(1)}, f32[1,192,768]{2,1,0:T(8,128)}, u32[]{:S(2)}) copy-start(f32[1,192,768]{2,1,0:T(8,128)} %param.16) | copy-start | bytes 1769476
  135.2 0.7 copy-start.10
Sparse Core Ops, SparseCore 0:
  35.3 42.4 all-reduce.3
  80.2 37.0 all-reduce.5
